TPU v7x, 32 devices: a whole 2x2x4 slice. The times are simulated.
32 devices in a mesh: dp: 16 (over z, y, x), tensor: 2 (over core).
Axes of the slice: x: 2, y: 2, z: 4, core: 2. Of those that a mesh axis runs over, the one named last changes fastest.
Arguments:
- inputs: bfloat16 [16, 1024, 768], P(None, 'dp', 'tensor'), may hold values from -6 to 6
- lengths: int32 [16], replicated, may hold values from 1 to 1024, 12288 in all
- order: int32 [16], replicated, may hold values from 0 to 15, each once
- w_query: bfloat16 [768, 768], P(None, 'tensor'), may hold values from -0.3125 to 0.3125
- b_query: bfloat16 [768], P('tensor'), may hold values from -3 to 3
- w_key: bfloat16 [768, 768], P(None, 'tensor'), may hold values from -0.3125 to 0.3125
- w_value: bfloat16 [768, 768], P(None, 'tensor'), may hold values from -0.21875 to 0.21875
- b_value: bfloat16 [768], P('tensor'), may hold values from -3 to 3
- w_out: bfloat16 [768, 768], P('tensor'), may hold values from -0.875 to 0.875
- b_out: bfloat16 [768], P('tensor'), may hold values from -3 to 3
- gain_one: bfloat16 [768], P('tensor'), may hold values from 0.5 to 1.5
- shift_one: bfloat16 [768], P('tensor'), may hold values from -3 to 3
- w_up: bfloat16 [768, 3072], P(None, 'tensor'), may hold values from -0.21875 to 0.21875
- b_up: bfloat16 [3072], P('tensor'), may hold values from -3 to 3
- w_down: bfloat16 [3072, 768], P('tensor'), may hold values from -0.109375 to 0.109375
- b_down: bfloat16 [768], P('tensor'), may hold values from -3 to 3
- gain_two: bfloat16 [768], P('tensor'), may hold values from 0.5 to 1.5
- shift_two: bfloat16 [768], P('tensor'), may hold values from -3 to 3
- cotangent: bfloat16 [16, 1024, 768], P('dp', 'tensor'), may hold values from -6 to 6
Outputs:
- output: bfloat16 [16, 1024, 768], P('dp', 'tensor')
- input_grad: bfloat16 [16, 1024, 768], P(None, 'dp', 'tensor')
- grad_w_query: float32 [768, 768], P(None, 'tensor')
- grad_b_query: float32 [768], P('tensor')
- grad_w_key: float32 [768, 768], P(None, 'tensor')
- grad_w_value: float32 [768, 768], P(None, 'tensor')
- grad_b_value: float32 [768], P('tensor')
- grad_w_out: float32 [768, 768], P('tensor')
- grad_b_out: float32 [768], P('tensor')
- grad_gain_one: float32 [768], P('tensor')
- grad_shift_one: float32 [768], P('tensor')
- grad_w_up: float32 [768, 3072], P(None, 'tensor')
- grad_b_up: float32 [3072], P('tensor')
- grad_w_down: float32 [3072, 768], P('tensor')
- grad_b_down: float32 [768], P('tensor')
- grad_gain_two: float32 [768], P('tensor')
- grad_shift_two: float32 [768], P('tensor')
Inputs may be any that keep to these rules, and one draw needn't show every extreme that they name: Valid tokens of each sequence; the first lengths entries of a sequence's 1024 slots hold its tokens, and some sequence fills all 1024. `order`: a permutation of the 16 sequences.
All inputs are finite; a program needn't handle non-finite values.
Results may differ from a plain program's by a relative error of at most 0.015.
The roundings to bfloat16 on the way count: a program that leaves them out, or rounds other values in their place, can miss the bound.
Values may be sent and summed in bfloat16 or wider, within the bound.
No kernel may reach another device: no remote copies, remote signals or barrier semaphores. Data moves between devices by JAX's collectives and lax.ppermute only.
A program may use at most 192 MiB of HBM per device.

v0:
```python
import jax
import jax.numpy as jnp
from jax import lax
from jax.sharding import PartitionSpec as P

HEAD_DIM = 64
epsilon = 1e-06
masked_score = -1e30


def layer_norm(value, gain, shift):
    center = value - jnp.mean(value, axis=-1, keepdims=True)
    spread = jnp.mean(center * center, axis=-1, keepdims=True)
    return center * lax.rsqrt(spread + epsilon) * gain + shift


def gelu_exact(value):
    return jax.nn.gelu(value, approximate=False)


def product(left, right, form):
    return jnp.einsum(form, left, right, preferred_element_type=jnp.float32)


def masked_scores(query, keys, length):
    span = query.shape[0]
    scores = product(query, keys, "qhd,khd->hqk") * query.shape[-1] ** (-0.5)
    valid = jnp.arange(span) < length
    return jnp.where(valid[None, None, :], scores, masked_score)


def attend_forward(packed):
    query, keys, values, length = packed
    scores = masked_scores(query, keys, length)
    top = jnp.max(scores, axis=-1, keepdims=True)
    weights = jnp.exp(scores - top)
    total = jnp.sum(weights, axis=-1, keepdims=True)
    probs_low = (weights / total).astype(jnp.bfloat16)
    mixed = product(probs_low, values, "hqk,khd->qhd")
    return (mixed, (top + jnp.log(total))[..., 0])


def attend_backward(packed):
    query, keys, values, length, log_total, grad_mixed = packed
    scale = query.shape[-1] ** (-0.5)
    scores = masked_scores(query, keys, length)
    probs = jnp.exp(scores - log_total[..., None])
    grad_values = product(probs.astype(jnp.bfloat16), grad_mixed, "hqk,qhd->khd")
    grad_probs = product(grad_mixed, values, "qhd,khd->hqk")
    inner = jnp.sum(grad_probs * probs, axis=-1, keepdims=True)
    grad_scores = (probs * (grad_probs - inner) * scale).astype(jnp.bfloat16)
    grad_query = product(grad_scores, keys, "hqk,khd->qhd")
    grad_keys = product(grad_scores, query, "hqk,qhd->khd")
    return (grad_query, grad_keys, grad_values)


def on_device(
    inputs,
    lengths,
    order,
    w_query,
    b_query,
    w_key,
    w_value,
    b_value,
    w_out,
    b_out,
    gain_one,
    shift_one,
    w_up,
    b_up,
    w_down,
    b_down,
    gain_two,
    shift_two,
    cotangent,
):
    dp_count = lax.axis_size("dp")
    seq_local = inputs.shape[0] // dp_count
    seq_len = inputs.shape[1] * dp_count
    half = seq_len // lax.axis_size("tensor")
    offset = lax.axis_index("tensor") * half
    width = w_query.shape[0]
    local_width = w_query.shape[1]
    local_heads = local_width // HEAD_DIM
    token_count = seq_local * seq_len
    head_shape = (seq_local, seq_len, local_heads, HEAD_DIM)
    factor = (order.shape[0] * seq_len) ** (-0.5)
    arranged = inputs[order]
    vectors = jnp.stack([b_out, gain_one, shift_one, b_down, gain_two, shift_two])[None]
    dealt_half = lax.all_to_all(arranged, "dp", split_axis=0, concat_axis=1, tiled=True)
    dealt, vectors_full = (
        lax.all_gather(dealt_half, "tensor", axis=2, tiled=True),
        lax.all_gather(vectors, "tensor", axis=2, tiled=True),
    )
    vectors_full = vectors_full[0].astype(jnp.float32)
    bias_out = vectors_full[0]
    gain_first = vectors_full[1]
    shift_first = vectors_full[2]
    bias_down = vectors_full[3]
    gain_second = vectors_full[4]
    shift_second = vectors_full[5]
    dealt_lengths = lax.dynamic_slice_in_dim(
        lengths[order], lax.axis_index("dp") * seq_local, seq_local
    )
    tokens_flat = dealt.reshape(token_count, width)
    query = (product(tokens_flat, w_query, "nd,df->nf") + b_query.astype(jnp.float32)).astype(
        jnp.bfloat16
    )
    keys = product(tokens_flat, w_key, "nd,df->nf").astype(jnp.bfloat16)
    values = (product(tokens_flat, w_value, "nd,df->nf") + b_value.astype(jnp.float32)).astype(
        jnp.bfloat16
    )
    query_heads = query.reshape(head_shape)
    key_heads = keys.reshape(head_shape)
    value_heads = values.reshape(head_shape)
    mixed, log_total = lax.map(attend_forward, (query_heads, key_heads, value_heads, dealt_lengths))
    mixed = mixed.astype(jnp.bfloat16).reshape(token_count, local_width)
    attention = product(mixed, w_out, "nh,hd->nd").reshape(seq_local, seq_len, width)
    attention = lax.psum_scatter(attention, "tensor", scatter_dimension=1, tiled=True)
    residual = lax.dynamic_slice_in_dim(dealt, offset, half, 1).astype(jnp.float32)
    normed, norm_one_back = jax.vjp(
        layer_norm, residual + attention + bias_out, gain_first, shift_first
    )
    normed_low = normed.astype(jnp.bfloat16)
    normed_all = lax.all_gather(normed_low, "tensor", axis=1, tiled=True)
    normed_rows = normed_all.reshape(token_count, width)
    upper = product(normed_rows, w_up, "nd,df->nf") + b_up.astype(jnp.float32)
    active, gelu_back = jax.vjp(gelu_exact, upper)
    active_low = active.astype(jnp.bfloat16)
    feed_terms = product(active_low, w_down, "nf,fd->nd").reshape(seq_local, seq_len, width)
    feed = lax.psum_scatter(feed_terms, "tensor", scatter_dimension=1, tiled=True)
    result, norm_two_back = jax.vjp(
        layer_norm, normed + feed + bias_down, gain_second, shift_second
    )
    output = result.astype(jnp.bfloat16)
    grad_two, grad_gain_two, grad_shift_two = norm_two_back(cotangent.astype(jnp.float32))
    grad_bias_down = jnp.sum(grad_two, axis=(0, 1))
    grad_two_low = grad_two.astype(jnp.bfloat16)
    grad_all = lax.all_gather(grad_two_low, "tensor", axis=1, tiled=True)
    grad_rows = grad_all.reshape(token_count, width)
    grad_active = product(grad_rows, w_down, "nd,fd->nf")
    (grad_upper,) = gelu_back(grad_active)
    grad_upper_low = grad_upper.astype(jnp.bfloat16)
    grad_w_up = product(normed_rows, grad_upper_low, "nd,nf->df")
    grad_b_up = jnp.sum(grad_upper, axis=0)
    grad_w_down = product(active_low, grad_rows, "nf,nd->fd")
    normed_terms = product(grad_upper_low, w_up, "nf,df->nd").reshape(seq_local, seq_len, width)
    grad_normed = lax.psum_scatter(normed_terms, "tensor", scatter_dimension=1, tiled=True)
    grad_one, grad_gain_one, grad_shift_one = norm_one_back(grad_normed + grad_two)
    grad_bias_out = jnp.sum(grad_one, axis=(0, 1))
    grad_one_all = lax.all_gather(
        grad_one.astype(jnp.bfloat16), "tensor", axis=1, tiled=True
    ).reshape(token_count, width)
    grad_w_out = product(mixed, grad_one_all, "nh,nd->hd")
    grad_mixed = product(grad_one_all, w_out, "nd,hd->nh").astype(jnp.bfloat16).reshape(head_shape)
    grad_query, grad_keys, grad_values = lax.map(
        attend_backward, (query_heads, key_heads, value_heads, dealt_lengths, log_total, grad_mixed)
    )
    grad_query = grad_query.astype(jnp.bfloat16).reshape(token_count, local_width)
    grad_keys = grad_keys.astype(jnp.bfloat16).reshape(token_count, local_width)
    grad_values = grad_values.astype(jnp.bfloat16).reshape(token_count, local_width)
    grad_w_query = product(tokens_flat, grad_query, "nd,nf->df")
    grad_b_query = jnp.sum(grad_query, axis=0, dtype=jnp.float32)
    grad_w_key = product(tokens_flat, grad_keys, "nd,nf->df")
    grad_w_value = product(tokens_flat, grad_values, "nd,nf->df")
    grad_b_value = jnp.sum(grad_values, axis=0, dtype=jnp.float32)
    grad_inputs = (
        product(grad_query, w_query, "nf,df->nd")
        + product(grad_keys, w_key, "nf,df->nd")
        + product(grad_values, w_value, "nf,df->nd")
    )
    grad_inputs = grad_inputs.reshape(seq_local, seq_len, width)
    own_rows = lax.dynamic_slice_in_dim(grad_inputs, offset, half, 1) + grad_one
    grad_inputs = lax.dynamic_update_slice_in_dim(grad_inputs, own_rows, offset, 1)
    vector_grads = jnp.stack(
        [
            grad_bias_out,
            grad_gain_one,
            grad_shift_one,
            grad_bias_down,
            grad_gain_two,
            grad_shift_two,
        ]
    )[None]
    grad_inputs, vector_grads = (
        lax.psum_scatter(
            grad_inputs.astype(jnp.bfloat16), "tensor", scatter_dimension=2, tiled=True
        ).astype(jnp.float32),
        lax.psum_scatter(
            vector_grads.astype(jnp.bfloat16), "tensor", scatter_dimension=2, tiled=True
        ).astype(jnp.float32),
    )
    returned = lax.all_to_all(
        grad_inputs.astype(jnp.bfloat16), "dp", split_axis=1, concat_axis=0, tiled=True
    )
    inverse = jnp.zeros_like(order).at[order].set(jnp.arange(order.shape[0], dtype=jnp.int32))
    input_grad = returned[inverse]
    summed = lax.psum(
        (
            grad_w_query,
            grad_b_query,
            grad_w_key,
            grad_w_value,
            grad_b_value,
            grad_w_out,
            grad_w_up,
            grad_b_up,
            grad_w_down,
            vector_grads,
        ),
        "dp",
    )
    vector_sums = summed[9][0] * factor
    return (
        output,
        input_grad,
        summed[0] * factor,
        summed[1] * factor,
        summed[2] * factor,
        summed[3] * factor,
        summed[4] * factor,
        summed[5] * factor,
        vector_sums[0],
        vector_sums[1],
        vector_sums[2],
        summed[6] * factor,
        summed[7] * factor,
        summed[8] * factor,
        vector_sums[3],
        vector_sums[4],
        vector_sums[5],
    )


def solution(mesh):
    return jax.shard_map(
        on_device,
        mesh=mesh,
        in_specs=(
            P(None, "dp", "tensor"),
            P(),
            P(),
            P(None, "tensor"),
            P("tensor"),
            P(None, "tensor"),
            P(None, "tensor"),
            P("tensor"),
            P("tensor", None),
            P("tensor"),
            P("tensor"),
            P("tensor"),
            P(None, "tensor"),
            P("tensor"),
            P("tensor", None),
            P("tensor"),
            P("tensor"),
            P("tensor"),
            P("dp", "tensor", None),
        ),
        out_specs=(
            P("dp", "tensor", None),
            P(None, "dp", "tensor"),
            P(None, "tensor"),
            P("tensor"),
            P(None, "tensor"),
            P(None, "tensor"),
            P("tensor"),
            P("tensor", None),
            P("tensor"),
            P("tensor"),
            P("tensor"),
            P(None, "tensor"),
            P("tensor"),
            P("tensor", None),
            P("tensor"),
            P("tensor"),
            P("tensor"),
        ),
        check_vma=False,
    )
```

profile of v0, /device:TPU:0, one launch (start us, length us, event | category | flops | bytes accessed | tf_op | source)
XLA Modules:
  0.0 789.3 jit_solution(8190659484800640758)
XLA Ops:
  8.6 1.8 gather_fusion
  10.5 29.5 %all_to_all.24 = bf16[16,64,384]{2,1,0:T(8,128)(2,1)} all-to-all(bf16[16,64,384]{2,1,0:T(8,128)(2,1)S(1)} %gather_fusion), channel_id=1, replica_groups=mesh['dp'=16,'tensor'=2] {'dp'}, dimensions={0} | all-to-all | bytes 1572864 | tf_op jit(solution)/shard_map/all_to_all | solution.py:91
  42.0 5.6 all-gather.6.cloned.1.call-done
  47.7 2.5 fusion.79
  50.2 0.8 add_convert_fusion.1
  51.0 10.6 %fusion.3 = (f32[6,1024]{1,0:T(8,128)S(1)}, f32[6,1024,1024]{1,2,0:T(8,128)}) fusion(pred[1024]{0:T(1024)(128)(4,1)S(1)} %iota_compare_fusion, bf16[1024,6,64]{0,2,1:T(8,128)(2,1)S(1)} %bitcast.140, bf16[1024,6,64]{0,2,1:T(8,128)(2,1)S(1)} %bitcast.138), kind=kOutput, calls=%fused_computation.13 | convolution fusion | flops 824174592 | bytes 26764288 | tf_op jit(solution)/shard_map/while/body/eval_jaxpr/qhd,khd->hqk/dot_general | solution.py:22
  61.6 11.8 %fusion.2 = f32[6,1024]{1,0:T(8,128)S(1)} fusion(f32[6,1024,1024]{1,2,0:T(8,128)} %get-tuple-element.112, f32[6,1024]{1,0:T(8,128)S(1)} %get-tuple-element.111, pred[1024]{0:T(1024)(128)(4,1)S(1)} %iota_compare_fusion), kind=kLoop, calls=%fused_computation.12 | loop fusion | flops 25159680 | bytes 25216000 | tf_op jit(solution)/shard_map/while/body/eval_jaxpr/reduce_sum | solution.py:37
  74.3 11.8 %fusion.91 = bf16[6,64,1024]{2,1,0:T(8,128)(2,1)S(1)} fusion(bf16[1024,6,64]{0,2,1:T(8,128)(2,1)S(1)} %bitcast.134, f32[6,1024,1024]{1,2,0:T(8,128)} %get-tuple-element.112, f32[6,1024]{1,0:T(8,128)S(1)} %fusion.2, f32[6,1024]{1,0:T(8,128)S(1)} %get-tuple-element.111, pred[1024]{0:T(1024)(128)(4,1)S(1)} %iota_compare_fusion), kind=kOutput, calls=%fused_computation.106 | convolution fusion | flops 837156864 | bytes 26788864 | tf_op jit(solution)/shard_map/while/body/eval_jaxpr/hqk,khd->qhd/dot_general | solution.py:22
  86.1 0.9 copy-done.21
  87.0 2.7 convolution_bitcast_fusion.2
  90.0 2.0 all-gather
  92.1 10.2 %reduce-scatter.10.cloned.1.call-done = f32[1,512,768]{2,1,0:T(8,128)} async-done(((f32[1,1024,768]{2,1,0:T(8,128)}), f32[1,512,768]{2,1,0:T(8,128)}) %reduce-scatter.10.cloned.1.call-update) | async-done | bytes 1572880 | tf_op jit(solution)/shard_map/reduce_scatter | solution.py:120
  102.2 1.9 fusion.115
  105.3 1.2 fusion.92
  106.6 11.2 %all-gather.8.cloned.1.call-done = bf16[1,1024,768]{2,1,0:T(8,128)(2,1)} async-done(((bf16[1,512,768]{2,1,0:T(8,128)(2,1)}), bf16[1,1024,768]{2,1,0:T(8,128)(2,1)}) %all-gather.8.cloned.1.call-update) | async-done | bytes 1572880 | tf_op jit(solution)/shard_map/all_gather | solution.py:126
  117.7 18.2 %multiply_convert_fusion.1 = (bf16[1024,1536]{1,0:T(8,128)(2,1)S(1)}, f32[1024,1536]{1,0:T(8,128)}, f32[1024,1536]{1,0:T(8,128)}) fusion(f32[1536]{0:T(1024)S(1)} %convert_element_type.127, bf16[768,1536]{1,0:T(8,128)(2,1)S(1)} %copy-done, bf16[1,1024,768]{2,1,0:T(8,128)(2,1)} %all-gather.8.cloned.1.call-done), kind=kOutput, calls=%fused_computation.31 | convolution fusion | flops 2519728128 | bytes 19666944 | tf_op jit(solution)/shard_map/nd,df->nf/dot_general | solution.py:22
  136.0 1.6 copy-done.48
  137.6 4.3 convolution_bitcast_fusion.1
  141.9 12.4 %reduce-scatter.12.cloned.1.call-done = f32[1,512,768]{2,1,0:T(8,128)} async-done(((f32[1,1024,768]{2,1,0:T(8,128)}), f32[1,512,768]{2,1,0:T(8,128)}) %reduce-scatter.12.cloned.1.call-update) | async-done | bytes 1572880 | tf_op jit(solution)/shard_map/reduce_scatter | solution.py:132
  154.4 2.5 fusion.113
  158.0 1.6 fusion.112
  159.6 1.1 copy-done.5
  160.7 1.1 add_reduce_fusion.1
  162.3 10.8 %all-gather.10.cloned.1.call-done = bf16[1,1024,768]{2,1,0:T(8,128)(2,1)} async-done(((bf16[1,512,768]{2,1,0:T(8,128)(2,1)}), bf16[1,1024,768]{2,1,0:T(8,128)(2,1)}) %all-gather.10.cloned.1.call-update) | async-done | bytes 1572880 | tf_op jit(solution)/shard_map/all_gather | solution.py:140
  173.1 10.2 %fusion.118 = (f32[1536]{0:T(1024)S(1)}, bf16[1024,1536]{1,0:T(8,128)(2,1)S(1)}) fusion(f32[1024,1536]{1,0:T(8,128)} %get-tuple-element.103, bf16[1536,768]{1,0:T(8,128)(2,1)} %param.33, bf16[1,1024,768]{2,1,0:T(8,128)(2,1)} %all-gather.10.cloned.1.call-done, f32[1024,1536]{1,0:T(8,128)} %get-tuple-element.113, f32[1536]{0:T(1024)S(1)} %convert_element_type.127), kind=kOutput, calls=%fused_computation.168 | convolution fusion | flops 2441083392 | bytes 19673088 | tf_op jit(solution)/shard_map/nd,fd->nf/dot_general | solution.py:22
  183.3 1.6 copy-done.10
  184.9 4.3 convolution_bitcast_fusion
  189.3 12.4 %reduce-scatter.14.cloned.1.call-done = f32[1,512,768]{2,1,0:T(8,128)} async-done(((f32[1,1024,768]{2,1,0:T(8,128)}), f32[1,512,768]{2,1,0:T(8,128)}) %reduce-scatter.14.cloned.1.call-update) | async-done | bytes 1572880 | tf_op jit(solution)/shard_map/reduce_scatter | solution.py:149
  201.8 2.7 multiply_reduce_fusion.1
  205.1 1.1 copy-done.6
  206.3 1.1 add_reduce_fusion
  207.4 11.2 %all-gather.12.cloned.1.call-done = bf16[1,1024,768]{2,1,0:T(8,128)(2,1)} async-done(((bf16[1,512,768]{2,1,0:T(8,128)(2,1)}), bf16[1,1024,768]{2,1,0:T(8,128)(2,1)}) %all-gather.12.cloned.1.call-update) | async-done | bytes 1572880 | tf_op jit(solution)/shard_map/all_gather | solution.py:152
  218.6 2.2 fusion.82
  220.8 10.2 %fusion.119 = f32[6,1024,1024]{1,2,0:T(8,128)} fusion(bf16[1024,6,64]{0,2,1:T(8,128)(2,1)S(1)} %bitcast.136, bf16[1024,6,64]{0,2,1:T(8,128)(2,1)S(1)} %bitcast.135), kind=kOutput, calls=%fused_computation.169 | convolution fusion | flops 805306368 | bytes 26738688 | tf_op jit(solution)/shard_map/while/body/eval_jaxpr/qhd,khd->hqk/dot_general | solution.py:22
  231.1 12.3 %convert_reduce_fusion = (f32[6,64]{1,0:T(8,128)S(1)}, bf16[6,64,1024]{2,1,0:T(8,128)(2,1)}) fusion(bf16[1024,6,64]{0,2,1:T(8,128)(2,1)S(1)} %bitcast.137, f32[6,1024,1024]{1,2,0:T(8,128)} %get-tuple-element.112, f32[6,1024]{1,0:T(8,128)S(1)} %log_add_fusion, pred[1024]{0:T(1024)(128)(4,1)S(1)} %iota_compare_fusion), kind=kOutput, calls=%fused_computation.88 | convolution fusion | flops 831651456 | bytes 26765824 | tf_op jit(solution)/shard_map/while/body/eval_jaxpr/hqk,qhd->khd/dot_general | solution.py:22
  243.4 34.1 %fusion.88 = bf16[6,64,1024]{2,1,0:T(8,128)(2,1)S(1)} fusion(bf16[1024,6,64]{0,2,1:T(8,128)(2,1)S(1)} %bitcast.141, f32[6,1024,1024]{1,2,0:T(8,128)} %fusion.119, f32[6,1024,1024]{1,2,0:T(8,128)} %get-tuple-element.112, f32[6,1024]{1,0:T(8,128)S(1)} %log_add_fusion, pred[1024]{0:T(1024)(128)(4,1)S(1)} %iota_compare_fusion), kind=kOutput, calls=%fused_computation.105 | convolution fusion | flops 874912768 | bytes 51930112 | tf_op jit(solution)/shard_map/while/body/eval_jaxpr/hqk,qhd->khd/dot_general | solution.py:22
  277.6 34.3 %convert_reduce_fusion.1 = (f32[6,64]{1,0:T(8,128)S(1)}, bf16[6,64,1024]{2,1,0:T(8,128)(2,1)S(1)}) fusion(bf16[1024,6,64]{0,2,1:T(8,128)(2,1)S(1)} %bitcast.139, f32[6,1024,1024]{1,2,0:T(8,128)} %fusion.119, f32[6,1024,1024]{1,2,0:T(8,128)} %get-tuple-element.112, f32[6,1024]{1,0:T(8,128)S(1)} %log_add_fusion, pred[1024]{0:T(1024)(128)(4,1)S(1)} %iota_compare_fusion), kind=kOutput, calls=%fused_computation.89 | convolution fusion | flops 875698816 | bytes 51931648 | tf_op jit(solution)/shard_map/while/body/eval_jaxpr/hqk,khd->qhd/dot_general | solution.py:22
  311.9 2.4 fusion.121
  314.3 1.0 fusion.120
  315.6 1.0 add_add_fusion
  316.9 1.2 copy-done.7
  318.5 5.6 copy.58
  324.1 3.6 copy.68
  328.0 7.4 fusion.48
  335.4 4.3 fusion.54
  341.3 3.2 fusion.44
  344.5 3.6 fusion.58
  348.1 2.0 fusion.62
  350.1 2.0 fusion.60
  352.2 3.1 reshape_bitcast_fusion
  355.3 5.0 copy.53
  360.9 5.4 reduce.43
  366.3 1.1 reshape.457
  367.4 6.8 all-to-all-start.1
  375.0 1.0 reshape_bitcast_fusion.1
  376.3 98.0 %all-reduce = (f32[384]{0:T(512)S(1)}, f32[384]{0:T(512)S(1)}, f32[1,6,384]{2,1,0:T(8,128)S(1)}, f32[1536]{0:T(1024)S(1)}) all-reduce(f32[384]{0:T(512)S(1)} %reduce_sum.220, f32[384]{0:T(512)S(1)} %reduce_sum.222, bf16[1,6,384]{2,1,0:T(8,128)(2,1)S(1)} %copy.61, ...), channel_id=1, replica_groups=mesh['dp'=16,'tensor'=2] {'dp'}, use_global_device_ids=true, to_apply=%region_18.19 | all-reduce | flops 4608 | bytes 32256 | tf_op jit(solution)/shard_map/psum | solution.py:199
  477.0 1.5 gather_fusion.2
  478.5 290.0 %all-reduce.4.cloned.1.call-done = (f32[768,384]{1,0:T(8,128)}, f32[768,384]{1,0:T(8,128)}, f32[768,384]{1,0:T(8,128)}, f32[384,768]{1,0:T(8,128)}, f32[768,1536]{1,0:T(8,128)}, /*index=5*/f32[1536,768]{1,0:T(8,128)}) async-done(((f32[768,384]{1,0:T(8,128)}, f32[768,384]{1,0:T(8,128)}, f32[768,384]{1,0:T(8,128)}, f32[384,768]{1,0:T(8,128)}, f32[768,1536]{1,0:T(8,128)}, /*index=5*/f32[1536,768]{1,0:T(8,128)}), ...) | async-done | bytes 14155792 | tf_op jit(solution)/shard_map/psum | solution.py:199
  768.5 2.5 broadcast_multiply_fusion.5
  771.0 2.4 broadcast_multiply_fusion.2
  773.3 2.9 broadcast_multiply_fusion.1
  776.2 1.0 slice-done
  777.4 2.7 broadcast_multiply_fusion
  780.1 1.6 broadcast_multiply_fusion.3
  (177 shorter events, 15.5 us)
Async XLA Ops:
  7.2 110.5 %copy-start = (bf16[768,1536]{1,0:T(8,128)(2,1)S(1)}, bf16[768,1536]{1,0:T(8,128)(2,1)}, u32[]{:S(2)}) copy-start(bf16[768,1536]{1,0:T(8,128)(2,1)} %param.31) | copy-start | bytes 7077892
  7.2 32.9 %copy-start.38 = (bf16[384]{0:T(512)(128)(2,1)S(1)}, bf16[384]{0:T(512)(128)(2,1)}, u32[]{:S(2)}) copy-start(bf16[384]{0:T(512)(128)(2,1)} %param.23) | copy-start | bytes 2308
  7.2 32.9 %copy-start.39 = (bf16[384]{0:T(512)(128)(2,1)S(1)}, bf16[384]{0:T(512)(128)(2,1)}, u32[]{:S(2)}) copy-start(bf16[384]{0:T(512)(128)(2,1)} %param.26) | copy-start | bytes 2308
  7.2 32.9 %copy-start.2 = (s32[16]{0:T(128)S(1)}, s32[16]{0:T(128)}, u32[]{:S(2)}) copy-start(s32[16]{0:T(128)} %param.20) | copy-start | bytes 196
  7.2 40.4 %all-gather.6.cloned.1.call-start = ((), (), s32[]{:S(2)}) async-start(), calls=%async_computation.7 | async-start | bytes 2359296 | tf_op jit(solution)/shard_map/all_gather | solution.py:93
  8.1 0.5 copy-start.46
  40.0 10.2 %copy-start.31 = (bf16[768,384]{1,0:T(8,128)(2,1)S(1)}, bf16[768,384]{1,0:T(8,128)(2,1)}, u32[]{:S(2)}) copy-start(bf16[768,384]{1,0:T(8,128)(2,1)} %param.22) | copy-start | bytes 1769476
  40.0 62.2 %reduce-scatter.10.cloned.1.call-start = ((), (), s32[]{:S(2)}) async-start(), calls=%async_computation.8 | async-start | bytes 4718592 | tf_op jit(solution)/shard_map/reduce_scatter | solution.py:120
  47.7 2.5 copy-start.35
  50.2 11.5 %copy-start.15 = (bf16[1024,384]{0,1:T(8,128)(2,1)}, bf16[1024,384]{0,1:T(8,128)(2,1)S(1)}, u32[]{:S(2)}) copy-start(bf16[1024,384]{0,1:T(8,128)(2,1)S(1)} %fusion.79) | copy-start | bytes 2359300
  51.0 10.6 %copy-start.17 = (bf16[1024,384]{0,1:T(8,128)(2,1)}, bf16[1024,384]{0,1:T(8,128)(2,1)S(1)}, u32[]{:S(2)}) copy-start(bf16[1024,384]{0,1:T(8,128)(2,1)S(1)} %add_convert_fusion.1) | copy-start | bytes 2359300
  61.6 11.8 %copy-start.33 = (bf16[768,384]{1,0:T(8,128)(2,1)S(1)}, bf16[768,384]{1,0:T(8,128)(2,1)}, u32[]{:S(2)}) copy-start(bf16[768,384]{1,0:T(8,128)(2,1)} %param.25) | copy-start | bytes 1769476
  74.2 11.9 %copy-start.13 = (bf16[1024,384]{0,1:T(8,128)(2,1)}, bf16[1024,384]{0,1:T(8,128)(2,1)S(1)}, u32[]{:S(2)}) copy-start(bf16[1024,384]{0,1:T(8,128)(2,1)S(1)} %add_convert_fusion.2) | copy-start | bytes 2359300
  74.3 12.7 %copy-start.29 = (bf16[384,768]{1,0:T(8,128)(2,1)S(1)}, bf16[384,768]{1,0:T(8,128)(2,1)}, u32[]{:S(2)}) copy-start(bf16[384,768]{1,0:T(8,128)(2,1)} %param.27) | copy-start | bytes 1769476
  86.1 0.9 copy-start.21
  87.0 2.8 copy-start.40
  87.0 2.8 copy-start.41
  87.0 2.8 copy-start.42
  87.0 2.9 copy-start.43
  87.0 2.9 copy-start.44
  87.0 2.9 copy-start.45
  89.8 28.0 %all-gather.8.cloned.1.call-start = ((), (), s32[]{:S(2)}) async-start(), calls=%async_computation.9 | async-start | bytes 2359296 | tf_op jit(solution)/shard_map/all_gather | solution.py:126
  104.1 1.1 copy-start.3
  104.1 2.4 copy-start.37
  106.5 47.9 %reduce-scatter.12.cloned.1.call-start = ((), (), s32[]{:S(2)}) async-start(), calls=%async_computation.10 | async-start | bytes 4718592 | tf_op jit(solution)/shard_map/reduce_scatter | solution.py:132
  117.7 19.9 %copy-start.47 = (bf16[1536,768]{1,0:T(8,128)(2,1)S(1)}, bf16[1536,768]{1,0:T(8,128)(2,1)}, u32[]{:S(2)}) copy-start(bf16[1536,768]{1,0:T(8,128)(2,1)} %param.33) | copy-start | bytes 7077892
  136.0 1.6 copy-start.48
  141.9 31.2 %all-gather.10.cloned.1.call-start = ((), (), s32[]{:S(2)}) async-start(), calls=%async_computation.11 | async-start | bytes 2359296 | tf_op jit(solution)/shard_map/all_gather | solution.py:140
  154.4 2.8 copy-start.8
  159.6 1.1 copy-start.5
  161.8 39.9 %reduce-scatter.14.cloned.1.call-start = ((), (), s32[]{:S(2)}) async-start(), calls=%async_computation.12 | async-start | bytes 4718592 | tf_op jit(solution)/shard_map/reduce_scatter | solution.py:149
  183.3 1.6 copy-start.10
  189.2 12.5 %copy-start.4 = (f32[1,512,768]{2,1,0:T(8,128)S(1)}, f32[1,512,768]{2,1,0:T(8,128)}, u32[]{:S(2)}) copy-start(f32[1,512,768]{2,1,0:T(8,128)} %copy-done.3) | copy-start | bytes 4718596
  189.3 29.3 %all-gather.12.cloned.1.call-start = ((), (), s32[]{:S(2)}) async-start(), calls=%async_computation.13 | async-start | bytes 2359296 | tf_op jit(solution)/shard_map/all_gather | solution.py:152
  204.5 14.1 %copy-start.30 = (bf16[384,768]{1,0:T(8,128)(2,1)S(1)}, bf16[384,768]{1,0:T(8,128)(2,1)}, u32[]{:S(2)}) copy-start(bf16[384,768]{1,0:T(8,128)(2,1)} %param.27) | copy-start | bytes 1769476
  205.1 1.1 copy-start.6
  206.3 14.6 %copy-start.14 = (bf16[1024,384]{0,1:T(8,128)(2,1)S(1)}, bf16[1024,384]{0,1:T(8,128)(2,1)}, u32[]{:S(2)}) copy-start(bf16[1024,384]{0,1:T(8,128)(2,1)} %copy-done.13) | copy-start | bytes 2359300
  207.4 144.8 %reduce-scatter.16.cloned.1.call-start = ((), (), s32[]{:S(2)}) async-start(), calls=%async_computation.14 | async-start | bytes 2359296
  231.1 12.4 %copy-start.18 = (bf16[1024,384]{0,1:T(8,128)(2,1)S(1)}, bf16[1024,384]{0,1:T(8,128)(2,1)}, u32[]{:S(2)}) copy-start(bf16[1024,384]{0,1:T(8,128)(2,1)} %copy-done.17) | copy-start | bytes 2359300
  243.4 34.2 %copy-start.16 = (bf16[1024,384]{0,1:T(8,128)(2,1)S(1)}, bf16[1024,384]{0,1:T(8,128)(2,1)}, u32[]{:S(2)}) copy-start(bf16[1024,384]{0,1:T(8,128)(2,1)} %copy-done.15) | copy-start | bytes 2359300
  277.6 34.3 %copy-start.23 = (bf16[6,64,1024]{2,1,0:T(8,128)(2,1)}, bf16[6,64,1024]{2,1,0:T(8,128)(2,1)S(1)}, u32[]{:S(2)}) copy-start(bf16[6,64,1024]{2,1,0:T(8,128)(2,1)S(1)} %fusion.88) | copy-start | bytes 2359300
  311.9 3.5 copy-start.25
  311.9 2.4 copy-start.32
  314.3 1.1 copy-start.27
  314.3 1.3 copy-start.34
  316.6 1.4 copy-start.7
  327.8 47.2 %reduce-scatter.18.cloned.1.call-start = ((), (), s32[]{:S(2)}) async-start(), calls=%async_computation.15 | async-start | bytes 294912
  328.0 7.4 copy-start.11
  328.0 7.4 copy-start.12
  335.4 5.9 copy-start.22
  339.8 4.7 copy-start.28
  341.0 427.5 %all-reduce.4.cloned.1.call-start = ((), (), s32[]{:S(2)}) async-start(), calls=%async_computation.16 | async-start | bytes 28311552 | tf_op jit(solution)/shard_map/psum | solution.py:199
  344.5 3.6 copy-start.26
  344.5 3.6 copy-start.36
  348.1 2.0 copy-start.24
  367.4 108.7 %all-to-all-start.1 = ((bf16[16,2,12288]{2,1,0:T(2,128)(2,1)}), bf16[16,2,12288]{2,1,0:T(2,128)(2,1)S(1)}, u32[]{:S(2)}, u32[]{:S(2)}) async-start(bf16[16,2,12288]{2,1,0:T(2,128)(2,1)} %reshape.457), calls=%async_computation.4 | async-start | bytes 1572864 | tf_op jit(solution)/shard_map/all_to_all | solution.py:194
  768.5 4.9 copy-start.9
  773.3 3.9 slice-start
  773.3 4.0 slice-start.1
  777.3 2.7 copy-start.19
  777.3 2.7 copy-start.20
  777.4 4.7 copy-start.1
Sparse Core Ops, SparseCore 0:
  40.1 7.4 all-gather.5
  89.9 12.3 reduce-scatter.9
  106.6 11.0 all-gather.7
  142.0 12.3 reduce-scatter.11
  162.0 11.0 all-gather.9
  189.4 12.3 reduce-scatter.13
  207.5 11.0 all-gather.11
  327.9 10.2 reduce-scatter.15
  341.1 8.8 reduce-scatter.17
  357.4 411.0 all-reduce.3
where the time goes:
time: 798 us; the launch traced here: 789 us
  waiting for transfers between devices  364 us (46%)
  matrix products  186 us (23%)
  blocking collectives  130 us (16%)
  other arithmetic  46.5 us (6%)
  local copies, waits for them, and re-layouts  39.5 us (5%)
  between operations  15.4 us (2%)
    psum x1, waiting for transfers between devices, on_device(): lax.psum((grad_w_query, grad_b_query, grad_w_key, grad_w_value, grad_b_va...  290 us
    dot_general x24, matrix products, product(): return jnp.einsum(form, left, right, preferred_element_type=jnp.float32)  186 us
    psum x1, blocking collectives, on_device(): lax.psum((grad_w_query, grad_b_query, grad_w_key, grad_w_value, grad_b_va...  98 us
    all_to_all x1, blocking collectives, on_device(): lax.all_to_all(arranged, 'dp', split_axis=0, concat_axis=1, tiled=True)  29.5 us
    unnamed x114, local copies, waits for them, and re-layouts  28.1 us
  transfers between devices with their start and end apart: 11, of which 8 were waited for; matrix products, arithmetic and copies ran while one was open for 6% of the time, Pallas kernels for 0%

commit v1 on v0

--- a/solution.py
+++ b/solution.py
@@ -6,6 +6,18 @@
 HEAD_DIM = 64
 epsilon = 1e-06
 masked_score = -1e30
+
+
+def in_blocks(array, dim, size):
+    dims = array.shape
+    blocks = array.reshape(*dims[:dim], size, dims[dim] // size, *dims[dim + 1 :])
+    return jnp.moveaxis(blocks, dim, 0)
+
+
+def laid_out(tiles, dim):
+    shape = list(tiles.shape[1:])
+    shape[dim] *= tiles.shape[0]
+    return jnp.moveaxis(tiles, 0, dim).reshape(shape)
 
 
 def layer_norm(value, gain, shift):
@@ -88,7 +100,15 @@
     factor = (order.shape[0] * seq_len) ** (-0.5)
     arranged = inputs[order]
     vectors = jnp.stack([b_out, gain_one, shift_one, b_down, gain_two, shift_two])[None]
-    dealt_half = lax.all_to_all(arranged, "dp", split_axis=0, concat_axis=1, tiled=True)
+    peers, index = (lax.axis_size("dp"), lax.axis_index("dp"))
+    blocks = in_blocks(arranged, 0, peers)
+    out = blocks
+    for step in range(1, peers):
+        target, source = ((index + step) % peers, (index - step) % peers)
+        sent = lax.dynamic_index_in_dim(blocks, target, 0)
+        other = lax.ppermute(sent, "dp", [(i, (i + step) % peers) for i in range(peers)])
+        out = lax.dynamic_update_slice_in_dim(out, other, source, axis=0)
+    dealt_half = laid_out(out, 1)
     dealt, vectors_full = (
         lax.all_gather(dealt_half, "tensor", axis=2, tiled=True),
         lax.all_gather(vectors, "tensor", axis=2, tiled=True),

time: 798 us -> 845 us (1.059)
  waiting for transfers between devices: 364 us -> 407 us
  starting transfers between devices: 7.87 us -> 40.7 us
  blocking collectives: 130 us -> 100 us
    ppermute x0 -> x15, waiting for transfers between devices: none -> 39.7 us  [on_device(): lax.ppermute(sent, 'dp', [(i, (i + step) % peers) for i in range(peers)])]
    ppermute x0 -> x15, starting transfers between devices: none -> 32.6 us  [on_device(): lax.ppermute(sent, 'dp', [(i, (i + step) % peers) for i in range(peers)])]
    all_to_all x1 -> x0, blocking collectives: 29.5 us -> none  [on_device(): lax.all_to_all(arranged, 'dp', split_axis=0, concat_axis=1, tiled=True)]
    unnamed x114 -> x116, local copies, waits for them, and re-layouts: 28.1 us -> 29 us
  transfers between devices with their start and end apart: 11 -> 26, of which waited for: 8 -> 18; matrix products, arithmetic and copies ran while one was open for 6% -> 6% of each run, Pallas kernels for 0% -> 0%
where the time goes in v1:
time: 845 us; the launch traced here: 842 us
  waiting for transfers between devices  407 us (48%)
  matrix products  187 us (22%)
  blocking collectives  100 us (12%)
  other arithmetic  46.4 us (5%)
  local copies, waits for them, and re-layouts  45.4 us (5%)
  starting transfers between devices  40.7 us (5%)
  between operations  15.7 us (2%)
    psum x1, waiting for transfers between devices, on_device(): lax.psum((grad_w_query, grad_b_query, grad_w_key, grad_w_value, grad_b_va...  290 us
    dot_general x24, matrix products, product(): return jnp.einsum(form, left, right, preferred_element_type=jnp.float32)  187 us
    psum x1, blocking collectives, on_device(): lax.psum((grad_w_query, grad_b_query, grad_w_key, grad_w_value, grad_b_va...  98.4 us
    ppermute x15, waiting for transfers between devices, on_device(): lax.ppermute(sent, 'dp', [(i, (i + step) % peers) for i in range(peers)])  39.7 us
    ppermute x15, starting transfers between devices, on_device(): lax.ppermute(sent, 'dp', [(i, (i + step) % peers) for i in range(peers)])  32.6 us
    unnamed x116, local copies, waits for them, and re-layouts  29 us
  transfers between devices with their start and end apart: 26, of which 18 were waited for; matrix products, arithmetic and copies ran while one was open for 6% of the time, Pallas kernels for 0%

profile of v1, /device:TPU:0, one launch (start us, length us, event | category | flops | bytes accessed | tf_op | source)
XLA Modules:
  0.0 841.6 jit_solution(6224944460485143574)
XLA Ops:
  8.6 1.8 gather_fusion
  11.3 3.0 collective-permute-start
  14.3 4.0 collective-permute-start.14
  18.3 2.0 collective-permute-start.13
  23.1 5.1 collective-permute-done.1
  28.2 7.0 collective-permute-done.2
  35.2 6.1 collective-permute-done.3
  41.3 1.9 collective-permute-start.4
  43.2 5.1 collective-permute-done.4
  49.9 4.5 collective-permute-done.5
  54.4 2.3 collective-permute-start.6
  56.7 3.8 collective-permute-done.6
  60.5 3.8 collective-permute-start.7
  64.3 2.5 collective-permute-done.7
  66.8 3.8 collective-permute-start.8
  70.6 2.1 collective-permute-done.8
  72.7 4.2 collective-permute-start.9
  77.0 1.7 collective-permute-done.9
  78.7 4.1 collective-permute-start.10
  82.8 1.7 collective-permute-done.10
  91.1 8.5 %all-gather.6.cloned.1.call-done = bf16[1,1024,768]{2,1,0:T(8,128)(2,1)} async-done(((bf16[1,1024,384]{2,1,0:T(8,128)(2,1)}), bf16[1,1024,768]{2,1,0:T(8,128)(2,1)}) %all-gather.6.cloned.1.call-update) | async-done | bytes 1572880 | tf_op jit(solution)/shard_map/all_gather | solution.py:113
  99.5 2.5 fusion.79
  102.9 10.6 %fusion.3 = (f32[6,1024]{1,0:T(8,128)S(1)}, f32[6,1024,1024]{1,2,0:T(8,128)}) fusion(pred[1024]{0:T(1024)(128)(4,1)S(1)} %iota_compare_fusion, bf16[1024,6,64]{0,2,1:T(8,128)(2,1)S(1)} %bitcast.172, bf16[1024,6,64]{0,2,1:T(8,128)(2,1)S(1)} %bitcast.170), kind=kOutput, calls=%fused_computation.13 | convolution fusion | flops 824174592 | bytes 26764288 | tf_op jit(solution)/shard_map/while/body/eval_jaxpr/qhd,khd->hqk/dot_general | solution.py:34
  113.5 11.8 %fusion.2 = f32[6,1024]{1,0:T(8,128)S(1)} fusion(f32[6,1024,1024]{1,2,0:T(8,128)} %get-tuple-element.127, f32[6,1024]{1,0:T(8,128)S(1)} %get-tuple-element.126, pred[1024]{0:T(1024)(128)(4,1)S(1)} %iota_compare_fusion), kind=kLoop, calls=%fused_computation.12 | loop fusion | flops 25159680 | bytes 25216000 | tf_op jit(solution)/shard_map/while/body/eval_jaxpr/reduce_sum | solution.py:49
  126.1 11.9 %fusion.91 = bf16[6,64,1024]{2,1,0:T(8,128)(2,1)S(1)} fusion(bf16[1024,6,64]{0,2,1:T(8,128)(2,1)S(1)} %bitcast.166, f32[6,1024,1024]{1,2,0:T(8,128)} %get-tuple-element.127, f32[6,1024]{1,0:T(8,128)S(1)} %fusion.2, f32[6,1024]{1,0:T(8,128)S(1)} %get-tuple-element.126, pred[1024]{0:T(1024)(128)(4,1)S(1)} %iota_compare_fusion), kind=kOutput, calls=%fused_computation.106 | convolution fusion | flops 837156864 | bytes 26788864 | tf_op jit(solution)/shard_map/while/body/eval_jaxpr/hqk,khd->qhd/dot_general | solution.py:34
  139.0 2.7 convolution_bitcast_fusion.2
  141.9 1.8 all-gather
  143.8 10.4 %reduce-scatter.10.cloned.1.call-done = f32[1,512,768]{2,1,0:T(8,128)} async-done(((f32[1,1024,768]{2,1,0:T(8,128)}), f32[1,512,768]{2,1,0:T(8,128)}) %reduce-scatter.10.cloned.1.call-update) | async-done | bytes 1572880 | tf_op jit(solution)/shard_map/reduce_scatter | solution.py:140
  154.2 1.9 fusion.115
  159.0 10.7 %all-gather.8.cloned.1.call-done = bf16[1,1024,768]{2,1,0:T(8,128)(2,1)} async-done(((bf16[1,512,768]{2,1,0:T(8,128)(2,1)}), bf16[1,1024,768]{2,1,0:T(8,128)(2,1)}) %all-gather.8.cloned.1.call-update) | async-done | bytes 1572880 | tf_op jit(solution)/shard_map/all_gather | solution.py:146
  169.7 18.2 %multiply_convert_fusion.1 = (bf16[1024,1536]{1,0:T(8,128)(2,1)S(1)}, f32[1024,1536]{1,0:T(8,128)}, f32[1024,1536]{1,0:T(8,128)}) fusion(f32[1536]{0:T(1024)S(1)} %convert_element_type.127, bf16[768,1536]{1,0:T(8,128)(2,1)S(1)} %copy-done, bf16[1,1024,768]{2,1,0:T(8,128)(2,1)} %all-gather.8.cloned.1.call-done), kind=kOutput, calls=%fused_computation.31 | convolution fusion | flops 2519728128 | bytes 19666944 | tf_op jit(solution)/shard_map/nd,df->nf/dot_general | solution.py:34
  189.5 4.3 convolution_bitcast_fusion.1
  193.8 12.4 %reduce-scatter.12.cloned.1.call-done = f32[1,512,768]{2,1,0:T(8,128)} async-done(((f32[1,1024,768]{2,1,0:T(8,128)}), f32[1,512,768]{2,1,0:T(8,128)}) %reduce-scatter.12.cloned.1.call-update) | async-done | bytes 1572880 | tf_op jit(solution)/shard_map/reduce_scatter | solution.py:152
  206.3 2.5 fusion.113
  213.8 11.2 %all-gather.10.cloned.1.call-done = bf16[1,1024,768]{2,1,0:T(8,128)(2,1)} async-done(((bf16[1,512,768]{2,1,0:T(8,128)(2,1)}), bf16[1,1024,768]{2,1,0:T(8,128)(2,1)}) %all-gather.10.cloned.1.call-update) | async-done | bytes 1572880 | tf_op jit(solution)/shard_map/all_gather | solution.py:160
  225.0 10.2 %fusion.118 = (f32[1536]{0:T(1024)S(1)}, bf16[1024,1536]{1,0:T(8,128)(2,1)S(1)}) fusion(f32[1024,1536]{1,0:T(8,128)} %get-tuple-element.103, bf16[1536,768]{1,0:T(8,128)(2,1)} %param.33, bf16[1,1024,768]{2,1,0:T(8,128)(2,1)} %all-gather.10.cloned.1.call-done, f32[1024,1536]{1,0:T(8,128)} %get-tuple-element.128, f32[1536]{0:T(1024)S(1)} %convert_element_type.127), kind=kOutput, calls=%fused_computation.198 | convolution fusion | flops 2441083392 | bytes 19673088 | tf_op jit(solution)/shard_map/nd,fd->nf/dot_general | solution.py:34
  236.9 4.3 convolution_bitcast_fusion
  241.2 12.4 %reduce-scatter.14.cloned.1.call-done = f32[1,512,768]{2,1,0:T(8,128)} async-done(((f32[1,1024,768]{2,1,0:T(8,128)}), f32[1,512,768]{2,1,0:T(8,128)}) %reduce-scatter.14.cloned.1.call-update) | async-done | bytes 1572880 | tf_op jit(solution)/shard_map/reduce_scatter | solution.py:169
  253.7 2.7 multiply_reduce_fusion.1
  259.4 11.2 %all-gather.12.cloned.1.call-done = bf16[1,1024,768]{2,1,0:T(8,128)(2,1)} async-done(((bf16[1,512,768]{2,1,0:T(8,128)(2,1)}), bf16[1,1024,768]{2,1,0:T(8,128)(2,1)}) %all-gather.12.cloned.1.call-update) | async-done | bytes 1572880 | tf_op jit(solution)/shard_map/all_gather | solution.py:172
  270.5 2.2 fusion.82
  272.8 10.2 %fusion.119 = f32[6,1024,1024]{1,2,0:T(8,128)} fusion(bf16[1024,6,64]{0,2,1:T(8,128)(2,1)S(1)} %bitcast.168, bf16[1024,6,64]{0,2,1:T(8,128)(2,1)S(1)} %bitcast.167), kind=kOutput, calls=%fused_computation.199 | convolution fusion | flops 805306368 | bytes 26738688 | tf_op jit(solution)/shard_map/while/body/eval_jaxpr/qhd,khd->hqk/dot_general | solution.py:34
  283.0 12.4 %convert_reduce_fusion = (f32[6,64]{1,0:T(8,128)S(1)}, bf16[6,64,1024]{2,1,0:T(8,128)(2,1)}) fusion(bf16[1024,6,64]{0,2,1:T(8,128)(2,1)S(1)} %bitcast.169, f32[6,1024,1024]{1,2,0:T(8,128)} %get-tuple-element.127, f32[6,1024]{1,0:T(8,128)S(1)} %log_add_fusion, pred[1024]{0:T(1024)(128)(4,1)S(1)} %iota_compare_fusion), kind=kOutput, calls=%fused_computation.88 | convolution fusion | flops 831651456 | bytes 26765824 | tf_op jit(solution)/shard_map/while/body/eval_jaxpr/hqk,qhd->khd/dot_general | solution.py:34
  295.4 34.1 %fusion.88 = bf16[6,64,1024]{2,1,0:T(8,128)(2,1)S(1)} fusion(bf16[1024,6,64]{0,2,1:T(8,128)(2,1)S(1)} %bitcast.173, f32[6,1024,1024]{1,2,0:T(8,128)} %fusion.119, f32[6,1024,1024]{1,2,0:T(8,128)} %get-tuple-element.127, f32[6,1024]{1,0:T(8,128)S(1)} %log_add_fusion, pred[1024]{0:T(1024)(128)(4,1)S(1)} %iota_compare_fusion), kind=kOutput, calls=%fused_computation.105 | convolution fusion | flops 874912768 | bytes 51930112 | tf_op jit(solution)/shard_map/while/body/eval_jaxpr/hqk,qhd->khd/dot_general | solution.py:34
  329.6 34.2 %convert_reduce_fusion.1 = (f32[6,64]{1,0:T(8,128)S(1)}, bf16[6,64,1024]{2,1,0:T(8,128)(2,1)S(1)}) fusion(bf16[1024,6,64]{0,2,1:T(8,128)(2,1)S(1)} %bitcast.171, f32[6,1024,1024]{1,2,0:T(8,128)} %fusion.119, f32[6,1024,1024]{1,2,0:T(8,128)} %get-tuple-element.127, f32[6,1024]{1,0:T(8,128)S(1)} %log_add_fusion, pred[1024]{0:T(1024)(128)(4,1)S(1)} %iota_compare_fusion), kind=kOutput, calls=%fused_computation.89 | convolution fusion | flops 875698816 | bytes 51931648 | tf_op jit(solution)/shard_map/while/body/eval_jaxpr/hqk,khd->qhd/dot_general | solution.py:34
  363.8 2.4 fusion.121
  370.4 5.6 copy.58
  376.0 3.6 copy.68
  380.0 7.4 fusion.48
  387.3 4.3 fusion.54
  393.2 3.2 fusion.44
  396.4 3.6 fusion.58
  400.0 2.0 fusion.62
  402.1 2.0 fusion.60
  404.2 3.1 reshape_bitcast_fusion
  407.3 5.0 copy.53
  412.8 5.4 reduce.43
  419.3 6.8 all-to-all-start
  428.2 98.4 %all-reduce = (f32[384]{0:T(512)S(1)}, f32[384]{0:T(512)S(1)}, f32[1,6,384]{2,1,0:T(8,128)S(1)}, f32[1536]{0:T(1024)S(1)}) all-reduce(f32[384]{0:T(512)S(1)} %reduce_sum.220, f32[384]{0:T(512)S(1)} %reduce_sum.222, bf16[1,6,384]{2,1,0:T(8,128)(2,1)S(1)} %copy.61, ...), channel_id=1, replica_groups=mesh['dp'=16,'tensor'=2] {'dp'}, use_global_device_ids=true, to_apply=%region_18.19 | all-reduce | flops 4608 | bytes 32256 | tf_op jit(solution)/shard_map/psum | solution.py:219
  530.9 289.8 %all-reduce.4.cloned.1.call-done = (f32[768,384]{1,0:T(8,128)}, f32[768,384]{1,0:T(8,128)}, f32[768,384]{1,0:T(8,128)}, f32[384,768]{1,0:T(8,128)}, f32[768,1536]{1,0:T(8,128)}, /*index=5*/f32[1536,768]{1,0:T(8,128)}) async-done(((f32[768,384]{1,0:T(8,128)}, f32[768,384]{1,0:T(8,128)}, f32[768,384]{1,0:T(8,128)}, f32[384,768]{1,0:T(8,128)}, f32[768,1536]{1,0:T(8,128)}, /*index=5*/f32[1536,768]{1,0:T(8,128)}), ...) | async-done | bytes 14155792 | tf_op jit(solution)/shard_map/psum | solution.py:219
  820.7 2.5 broadcast_multiply_fusion.5
  823.2 2.4 broadcast_multiply_fusion.2
  825.6 2.9 broadcast_multiply_fusion.1
  829.6 2.7 broadcast_multiply_fusion
  (224 shorter events, 46.7 us)
Async XLA Ops:
  7.2 162.5 %copy-start = (bf16[768,1536]{1,0:T(8,128)(2,1)S(1)}, bf16[768,1536]{1,0:T(8,128)(2,1)}, u32[]{:S(2)}) copy-start(bf16[768,1536]{1,0:T(8,128)(2,1)} %param.31) | copy-start | bytes 7077892
  7.2 81.9 %copy-start.39 = (bf16[384]{0:T(512)(128)(2,1)S(1)}, bf16[384]{0:T(512)(128)(2,1)}, u32[]{:S(2)}) copy-start(bf16[384]{0:T(512)(128)(2,1)} %param.23) | copy-start | bytes 2308
  7.2 81.9 %copy-start.40 = (bf16[384]{0:T(512)(128)(2,1)S(1)}, bf16[384]{0:T(512)(128)(2,1)}, u32[]{:S(2)}) copy-start(bf16[384]{0:T(512)(128)(2,1)} %param.26) | copy-start | bytes 2308
  7.2 81.9 %copy-start.2 = (s32[16]{0:T(128)S(1)}, s32[16]{0:T(128)}, u32[]{:S(2)}) copy-start(s32[16]{0:T(128)} %param.20) | copy-start | bytes 196
  7.2 92.3 %all-gather.6.cloned.1.call-start = ((), (), s32[]{:S(2)}) async-start(), calls=%async_computation.6 | async-start | bytes 2359296 | tf_op jit(solution)/shard_map/all_gather | solution.py:113
  11.3 9.9 %collective-permute-start = (bf16[1,1,64,384]{3,2,0,1:T(8,128)(2,1)}, bf16[1,1,64,384]{3,2,0,1:T(8,128)(2,1)}, u32[]{:S(2)}, u32[]{:S(2)}) collective-permute-start(bf16[1,1,64,384]{3,2,0,1:T(8,128)(2,1)} %get-tuple-element.125), channel_id=1, source_target_pairs={{0,2},{2,4},{4,6},{6,8},{8,10},{10,12},{12,14},{14,16},{16,18},{18... | collective-permute-start | bytes 147464 | tf_op jit(solution)/shard_map/ppermute | solution.py:109
  14.3 72.8 %collective-permute-start.14 = (bf16[1,1,64,384]{3,2,0,1:T(8,128)(2,1)S(1)}, bf16[1,1,64,384]{3,2,0,1:T(8,128)(2,1)}, u32[]{:S(2)}, u32[]{:S(2)}) collective-permute-start(bf16[1,1,64,384]{3,2,0,1:T(8,128)(2,1)S(1)} %get-tuple-element.111), channel_id=1, source_target_pairs={{0,30},{2,0},{4,2},{6,4},{8,6},{10,8},{12,10},{14,12},{16,14},{18,... | collective-permute-start | bytes 147464 | tf_op jit(solution)/shard_map/ppermute | solution.py:109
  18.3 68.0 %collective-permute-start.13 = (bf16[1,1,64,384]{3,2,0,1:T(8,128)(2,1)S(1)}, bf16[1,1,64,384]{3,2,0,1:T(8,128)(2,1)}, u32[]{:S(2)}, u32[]{:S(2)}) collective-permute-start(bf16[1,1,64,384]{3,2,0,1:T(8,128)(2,1)S(1)} %get-tuple-element.112), channel_id=1, source_target_pairs={{0,28},{2,30},{4,0},{6,2},{8,4},{10,6},{12,8},{14,10},{16,12},{18,... | collective-permute-start | bytes 147464 | tf_op jit(solution)/shard_map/ppermute | solution.py:109
  20.3 65.1 %collective-permute-start.12 = (bf16[1,1,64,384]{3,2,0,1:T(8,128)(2,1)S(1)}, bf16[1,1,64,384]{3,2,0,1:T(8,128)(2,1)}, u32[]{:S(2)}, u32[]{:S(2)}) collective-permute-start(bf16[1,1,64,384]{3,2,0,1:T(8,128)(2,1)S(1)} %get-tuple-element.113), channel_id=1, source_target_pairs={{0,26},{2,28},{4,30},{6,0},{8,2},{10,4},{12,6},{14,8},{16,10},{18,... | collective-permute-start | bytes 147464 | tf_op jit(solution)/shard_map/ppermute | solution.py:109
  20.8 63.8 %collective-permute-start.11 = (bf16[1,1,64,384]{3,2,0,1:T(8,128)(2,1)S(1)}, bf16[1,1,64,384]{3,2,0,1:T(8,128)(2,1)}, u32[]{:S(2)}, u32[]{:S(2)}) collective-permute-start(bf16[1,1,64,384]{3,2,0,1:T(8,128)(2,1)S(1)} %get-tuple-element.114), channel_id=1, source_target_pairs={{0,24},{2,26},{4,28},{6,30},{8,0},{10,2},{12,4},{14,6},{16,8},{18,... | collective-permute-start | bytes 147464 | tf_op jit(solution)/shard_map/ppermute | solution.py:109
  21.2 7.0 collective-permute-start.1
  28.2 7.0 collective-permute-start.2
  35.2 6.1 collective-permute-start.3
  41.3 7.0 collective-permute-start.4
  48.3 6.1 collective-permute-start.5
  54.4 6.1 collective-permute-start.6
  60.5 6.3 collective-permute-start.7
  66.8 5.9 collective-permute-start.8
  72.7 6.0 collective-permute-start.9
  78.7 5.9 collective-permute-start.10
  88.8 13.2 %copy-start.32 = (bf16[768,384]{1,0:T(8,128)(2,1)S(1)}, bf16[768,384]{1,0:T(8,128)(2,1)}, u32[]{:S(2)}) copy-start(bf16[768,384]{1,0:T(8,128)(2,1)} %param.22) | copy-start | bytes 1769476
  88.8 65.4 %reduce-scatter.10.cloned.1.call-start = ((), (), s32[]{:S(2)}) async-start(), calls=%async_computation.7 | async-start | bytes 4718592 | tf_op jit(solution)/shard_map/reduce_scatter | solution.py:140
  102.0 11.5 %copy-start.16 = (bf16[1024,384]{0,1:T(8,128)(2,1)}, bf16[1024,384]{0,1:T(8,128)(2,1)S(1)}, u32[]{:S(2)}) copy-start(bf16[1024,384]{0,1:T(8,128)(2,1)S(1)} %fusion.79) | copy-start | bytes 2359300
  102.9 10.6 %copy-start.18 = (bf16[1024,384]{0,1:T(8,128)(2,1)}, bf16[1024,384]{0,1:T(8,128)(2,1)S(1)}, u32[]{:S(2)}) copy-start(bf16[1024,384]{0,1:T(8,128)(2,1)S(1)} %add_convert_fusion.1) | copy-start | bytes 2359300
  113.5 11.8 %copy-start.34 = (bf16[768,384]{1,0:T(8,128)(2,1)S(1)}, bf16[768,384]{1,0:T(8,128)(2,1)}, u32[]{:S(2)}) copy-start(bf16[768,384]{1,0:T(8,128)(2,1)} %param.25) | copy-start | bytes 1769476
  126.1 11.9 %copy-start.14 = (bf16[1024,384]{0,1:T(8,128)(2,1)}, bf16[1024,384]{0,1:T(8,128)(2,1)S(1)}, u32[]{:S(2)}) copy-start(bf16[1024,384]{0,1:T(8,128)(2,1)S(1)} %add_convert_fusion.2) | copy-start | bytes 2359300
  126.1 12.8 %copy-start.30 = (bf16[384,768]{1,0:T(8,128)(2,1)S(1)}, bf16[384,768]{1,0:T(8,128)(2,1)}, u32[]{:S(2)}) copy-start(bf16[384,768]{1,0:T(8,128)(2,1)} %param.27) | copy-start | bytes 1769476
  138.9 2.8 copy-start.41
  138.9 2.8 copy-start.42
  138.9 2.8 copy-start.43
  138.9 2.9 copy-start.44
  138.9 2.9 copy-start.45
  138.9 2.9 copy-start.46
  141.7 28.0 %all-gather.8.cloned.1.call-start = ((), (), s32[]{:S(2)}) async-start(), calls=%async_computation.8 | async-start | bytes 2359296 | tf_op jit(solution)/shard_map/all_gather | solution.py:146
  156.1 2.9 copy-start.38
  158.4 47.8 %reduce-scatter.12.cloned.1.call-start = ((), (), s32[]{:S(2)}) async-start(), calls=%async_computation.9 | async-start | bytes 4718592 | tf_op jit(solution)/shard_map/reduce_scatter | solution.py:152
  169.6 19.9 %copy-start.48 = (bf16[1536,768]{1,0:T(8,128)(2,1)S(1)}, bf16[1536,768]{1,0:T(8,128)(2,1)}, u32[]{:S(2)}) copy-start(bf16[1536,768]{1,0:T(8,128)(2,1)} %param.33) | copy-start | bytes 7077892
  193.8 31.2 %all-gather.10.cloned.1.call-start = ((), (), s32[]{:S(2)}) async-start(), calls=%async_computation.10 | async-start | bytes 2359296 | tf_op jit(solution)/shard_map/all_gather | solution.py:160
  206.3 2.8 copy-start.8
  213.8 39.9 %reduce-scatter.14.cloned.1.call-start = ((), (), s32[]{:S(2)}) async-start(), calls=%async_computation.11 | async-start | bytes 4718592 | tf_op jit(solution)/shard_map/reduce_scatter | solution.py:169
  241.2 12.5 %copy-start.4 = (f32[1,512,768]{2,1,0:T(8,128)S(1)}, f32[1,512,768]{2,1,0:T(8,128)}, u32[]{:S(2)}) copy-start(f32[1,512,768]{2,1,0:T(8,128)} %copy-done.3) | copy-start | bytes 4718596
  241.2 29.4 %all-gather.12.cloned.1.call-start = ((), (), s32[]{:S(2)}) async-start(), calls=%async_computation.12 | async-start | bytes 2359296 | tf_op jit(solution)/shard_map/all_gather | solution.py:172
  256.4 14.1 %copy-start.31 = (bf16[384,768]{1,0:T(8,128)(2,1)S(1)}, bf16[384,768]{1,0:T(8,128)(2,1)}, u32[]{:S(2)}) copy-start(bf16[384,768]{1,0:T(8,128)(2,1)} %param.27) | copy-start | bytes 1769476
  258.2 14.6 %copy-start.15 = (bf16[1024,384]{0,1:T(8,128)(2,1)S(1)}, bf16[1024,384]{0,1:T(8,128)(2,1)}, u32[]{:S(2)}) copy-start(bf16[1024,384]{0,1:T(8,128)(2,1)} %copy-done.14) | copy-start | bytes 2359300
  259.3 144.9 %reduce-scatter.16.cloned.1.call-start = ((), (), s32[]{:S(2)}) async-start(), calls=%async_computation.13 | async-start | bytes 2359296
  283.0 12.4 %copy-start.19 = (bf16[1024,384]{0,1:T(8,128)(2,1)S(1)}, bf16[1024,384]{0,1:T(8,128)(2,1)}, u32[]{:S(2)}) copy-start(bf16[1024,384]{0,1:T(8,128)(2,1)} %copy-done.18) | copy-start | bytes 2359300
  295.4 34.2 %copy-start.17 = (bf16[1024,384]{0,1:T(8,128)(2,1)S(1)}, bf16[1024,384]{0,1:T(8,128)(2,1)}, u32[]{:S(2)}) copy-start(bf16[1024,384]{0,1:T(8,128)(2,1)} %copy-done.16) | copy-start | bytes 2359300
  329.5 34.3 %copy-start.24 = (bf16[6,64,1024]{2,1,0:T(8,128)(2,1)}, bf16[6,64,1024]{2,1,0:T(8,128)(2,1)S(1)}, u32[]{:S(2)}) copy-start(bf16[6,64,1024]{2,1,0:T(8,128)(2,1)S(1)} %fusion.88) | copy-start | bytes 2359300
  363.8 3.5 copy-start.26
  379.7 47.2 %reduce-scatter.18.cloned.1.call-start = ((), (), s32[]{:S(2)}) async-start(), calls=%async_computation.14 | async-start | bytes 294912
  380.0 7.4 copy-start.12
  380.0 7.4 copy-start.13
  387.3 5.9 copy-start.23
  391.7 4.7 copy-start.29
  392.9 427.8 %all-reduce.4.cloned.1.call-start = ((), (), s32[]{:S(2)}) async-start(), calls=%async_computation.15 | async-start | bytes 28311552 | tf_op jit(solution)/shard_map/psum | solution.py:219
  396.4 3.6 copy-start.27
  396.4 3.6 copy-start.37
  419.3 109.1 %all-to-all-start = ((bf16[16,2,12288]{2,1,0:T(2,128)(2,1)}), bf16[16,2,12288]{2,1,0:T(2,128)(2,1)S(1)}, u32[]{:S(2)}, u32[]{:S(2)}) async-start(bf16[16,2,12288]{2,1,0:T(2,128)(2,1)} %reshape.473), calls=%async_computation.3 | async-start | bytes 1572864 | tf_op jit(solution)/shard_map/all_to_all | solution.py:214
  820.7 4.9 copy-start.10
  825.6 3.9 slice-start
  825.6 4.0 slice-start.1
  829.6 2.7 copy-start.20
  829.6 2.7 copy-start.21
  829.6 4.7 copy-start.1
  (14 other events, 19.8 us)
Sparse Core Ops, SparseCore 0:
  88.9 10.5 all-gather.5
  141.8 12.3 reduce-scatter.9
  158.5 11.0 all-gather.7
  193.9 12.3 reduce-scatter.11
  213.9 11.0 all-gather.9
  241.3 12.3 reduce-scatter.13
  259.4 11.0 all-gather.11
  379.8 10.2 reduce-scatter.15
  393.0 8.7 reduce-scatter.17
  409.3 411.3 all-reduce.3
